TPU v7x, 32 devices: a whole 2x2x4 slice. The times are simulated.
32 devices in a mesh: groups: 2 (over y), ctx: 16 (over z, x, core).
Axes of the slice: x: 2, y: 2, z: 4, core: 2. Of those that a mesh axis runs over, the one named last changes fastest.
Arguments:
- queries: bfloat16 [512, 6144], P(('groups', 'ctx')), parts along dimension 0, may hold values from -8 to 8
- latents: bfloat16 [4096, 576], P(('groups', 'ctx')), parts along dimension 0, may hold values from -8 to 8
- w_uk: bfloat16 [32, 128, 512], replicated, may hold values from -0.5 to 0.5
- w_uv: bfloat16 [32, 512, 128], replicated, may hold values from -1.5 to 1.5
Outputs:
- attended: bfloat16 [512, 4096], P(('groups', 'ctx')), parts along dimension 0
There are 2 independent parts, one for each index of `groups`. A program takes and returns all parts, laid end to end along the dimension named above; an argument that names none is the same for every part. Nothing has to cross between parts.
All inputs are finite; a program needn't handle non-finite values.
Results may differ from a plain program's by a relative error of at most 0.008.
Values may be sent and summed in bfloat16 or wider, within the bound.
No kernel may reach another device: no remote copies, remote signals or barrier semaphores. Data moves between devices by JAX's collectives and lax.ppermute only.
A program may use at most 128 MiB of HBM per device.

v0:
```python
import math
import jax
import jax.numpy as jnp
from jax import lax
from jax.sharding import PartitionSpec as P

NOPE = 128
ROPE = 64
RANK = 512
VDIM = 128


def body(queries, latents, w_uk, w_uv):
    index = lax.axis_index("ctx")
    qrows = queries.shape[0]
    krows = latents.shape[0]
    offset = krows - qrows
    heads = w_uk.shape[0]
    query_pos = index * krows + offset + jnp.arange(qrows, dtype=jnp.int32)
    shaped = queries.reshape(qrows, heads, NOPE + ROPE)
    q_lat = jnp.einsum(
        "thi,hil->thl", shaped[:, :, :NOPE], w_uk, preferred_element_type=jnp.float32
    ).astype(jnp.bfloat16)
    q_rope = shaped[:, :, NOPE:]
    scale = 1.0 / jnp.sqrt(jnp.float32(NOPE + ROPE))
    last_query = jnp.max(query_pos)

    def inner(state, block, kstart):
        sub = block.shape[0]
        kpos = kstart + jnp.arange(sub, dtype=jnp.int32)

        def work(carried):
            running, total, acc = carried
            score = jnp.einsum(
                "thl,jl->thj", q_lat, block[:, :RANK], preferred_element_type=jnp.float32
            )
            score = score + jnp.einsum(
                "thr,jr->thj", q_rope, block[:, RANK:], preferred_element_type=jnp.float32
            )
            score = score * scale
            allowed = kpos[None, None, :] <= query_pos[:, None, None]
            score = jnp.where(allowed, score, -jnp.inf)
            fresh = jnp.maximum(running, jnp.max(score, axis=-1))
            expo = jnp.exp(score - fresh[:, :, None])
            factor = jnp.exp(running - fresh)
            total = total * factor + jnp.sum(expo, axis=-1)
            acc = acc * factor[:, :, None] + jnp.einsum(
                "thj,jl->thl",
                expo.astype(jnp.bfloat16),
                block[:, :RANK],
                preferred_element_type=jnp.float32,
            )
            return (fresh, total, acc)

        return lax.cond(kstart > last_query, lambda carried: carried, work, state)

    def accumulate(carry, piece, start):
        count = piece.shape[0]
        sub = math.gcd(count, 2048)
        if sub == count:
            return inner(carry, piece, start)
        blocks = piece.reshape(count // sub, sub, piece.shape[1])
        starts = start + jnp.arange(count // sub, dtype=jnp.int32) * sub

        def step(state, items):
            return (inner(state, items[0], items[1]), None)

        result, unused = lax.scan(step, carry, (blocks, starts))
        return result

    init = (
        jnp.full((qrows, heads), -1e30, jnp.float32),
        jnp.zeros((qrows, heads), jnp.float32),
        jnp.zeros((qrows, heads, RANK), jnp.float32),
    )
    running, total, acc = accumulate(
        init, lax.all_gather(latents, "ctx", axis=0, tiled=True), jnp.int32(0)
    )
    o_lat = (acc / total[:, :, None]).astype(jnp.bfloat16)
    result = jnp.einsum("thl,hlc->thc", o_lat, w_uv, preferred_element_type=jnp.float32).astype(
        jnp.bfloat16
    )
    result = result.reshape(qrows, heads * VDIM)
    return result


def solution(mesh):
    placed = (P(("groups", "ctx"), None), P(("groups", "ctx"), None), P(), P())
    return jax.shard_map(
        body, mesh=mesh, in_specs=placed, out_specs=P(("groups", "ctx"), None), check_vma=False
    )
```

profile of v0, /device:TPU:0, one launch (start us, length us, event | category | flops | bytes accessed | tf_op | source)
XLA Modules:
  0.0 76.3 jit_solution(9675604063775418156)
XLA Ops:
  6.5 0.0 all-gather.2.cloned.1.call-start
  6.5 1.7 %copy.11 = bf16[128,576]{1,0:T(8,128)(2,1)} copy(bf16[128,576]{0,1:T(8,128)(2,1)} %param.7) | data formatting | bytes 294912 | tf_op args[1]
  8.2 0.0 all-gather.2.cloned.1.call-update
  8.3 0.6 fusion.22
  9.6 1.3 %reshape.42 = bf16[16,32,192]{2,1,0:T(8,128)(2,1)S(1)} reshape(bf16[16,6144]{1,0:T(8,128)(2,1)} %param.6) | data formatting | bytes 393216 | tf_op jit(solution)/shard_map/reshape | solution.py:20
  10.9 2.9 %fusion.18 = bf16[16,32,512]{2,0,1:T(8,128)(2,1)S(1)} fusion(bf16[32,128,512]{2,1,0:T(8,128)(2,1)} %param.8, bf16[16,32,128]{2,1,0:T(8,128)(2,1)S(1)} %slice.16), kind=kOutput, calls=%fused_computation.20 | convolution fusion | flops 67371008 | bytes 4849664 | tf_op jit(solution)/shard_map/thi,hil->thl/dot_general | solution.py:21
  13.7 41.7 %all-gather.2.cloned.1.call-done = bf16[2048,576]{1,0:T(8,128)(2,1)} async-done(((bf16[128,576]{1,0:T(8,128)(2,1)}), bf16[2048,576]{1,0:T(8,128)(2,1)}) %all-gather.2.cloned.1.call-update) | async-done | bytes 2359312 | tf_op jit(solution)/shard_map/all_gather | solution.py:77
  55.4 10.1 %conditional.1 = (f32[16,32]{1,0:T(8,128)S(1)}, f32[16,32,512]{2,1,0:T(8,128)S(1)}) conditional(s32[]{:T(128)} %convert_element_type.21, (s32[2048]{0:T(1024)S(1)}, s32[16]{0:T(128)S(1)}, bf16[2048,576]{1,0:T(8,128)(2,1)}, bf16[16,32,512]{2,0,1:T(8,128)(2,1)S(1)}, bf16[16,32,192]{2,1,0:T(8,128)(2,1)S(1)}) %tuple.13, () %tuple.14), branch_computations={%region_1.4_spmd, %region_4.5_spmd} | conditional | flops 2290386432 | bytes 41396332 | solution.py:55
  55.4 0.0 copy-start
  55.4 0.1 broadcast_compare_fusion
  55.5 4.6 %copy.10 = bf16[2048,576]{0,1:T(8,128)(2,1)} copy(bf16[2048,576]{1,0:T(8,128)(2,1)} %get-tuple-element.19) | data formatting | bytes 4718592 | tf_op jit(solution)/shard_map
  60.1 0.0 copy-done
  60.1 1.4 %fusion.5 = f32[16,32,2048]{2,1,0:T(8,128)S(1)} fusion(bf16[2048,576]{1,0:T(8,128)(2,1)S(1)} %copy-done, bf16[16,32,512]{2,0,1:T(8,128)(2,1)S(1)} %get-tuple-element.33), kind=kOutput, calls=%fused_computation.6 | convolution fusion | flops 1073741824 | bytes 6815744 | tf_op jit(solution)/shard_map/cond/branch_0_fun/thl,jl->thj/dot_general | solution.py:34
  61.5 2.0 %fusion.23 = (f32[16,32]{1,0:T(8,128)S(1)}, f32[16,32,2048]{2,1,0:T(8,128)S(1)}) fusion(f32[16,32,2048]{2,1,0:T(8,128)S(1)} %fusion.5, bf16[2048,576]{0,1:T(8,128)(2,1)} %copy.10, bf16[16,32,192]{2,1,0:T(8,128)(2,1)S(1)} %get-tuple-element.20, pred[16,2048]{1,0:T(8,128)(4,1)S(1)} %broadcast_compare_fusion), kind=kOutput, calls=%fused_computation.29 | convolution fusion | flops 138411520 | bytes 8816640 | tf_op jit(solution)/shard_map/cond/branch_0_fun/thr,jr->thj/dot_general | solution.py:37
  63.4 0.7 fusion.1
  64.2 1.3 %fusion.10 = f32[16,32,512]{2,1,0:T(8,128)S(1)} fusion(bf16[2048,576]{1,0:T(8,128)(2,1)S(1)} %copy-done, f32[16,32,2048]{2,1,0:T(8,128)S(1)} %get-tuple-element.38, f32[16,32]{1,0:T(8,128)S(1)} %broadcast_maximum_fusion, f32[16,32]{1,0:T(8,128)S(1)} %get-tuple-element.35), kind=kOutput, calls=%fused_computation.11 | convolution fusion | flops 1076101120 | bytes 7356416 | tf_op jit(solution)/shard_map/cond/branch_0_fun/thj,jl->thl/dot_general | solution.py:47
  65.5 0.1 divide_convert_fusion
  65.7 3.1 %fusion.19 = bf16[32,2,8,128]{3,2,1,0:T(8,128)(2,1)S(1)} fusion(bf16[32,512,128]{2,1,0:T(8,128)(2,1)} %param.9, bf16[16,32,512]{2,1,0:T(8,128)(2,1)S(1)} %divide_convert_fusion), kind=kOutput, calls=%fused_computation.22 | convolution fusion | flops 67174400 | bytes 4849664 | tf_op jit(solution)/shard_map/thl,hlc->thc/dot_general | solution.py:80
  68.7 0.7 copy.25
  (5 shorter events, 0.1 us)
Async XLA Ops:
  6.5 48.9 %all-gather.2.cloned.1.call-start = ((), (), s32[]{:S(2)}) async-start(), calls=%async_computation | async-start | bytes 2785280 | tf_op jit(solution)/shard_map/all_gather | solution.py:77
  55.4 4.6 %copy-start = (bf16[2048,576]{1,0:T(8,128)(2,1)S(1)}, bf16[2048,576]{1,0:T(8,128)(2,1)}, u32[]{:S(2)}) copy-start(bf16[2048,576]{1,0:T(8,128)(2,1)} %get-tuple-element.19) | copy-start | bytes 7077892 | tf_op jit(solution)/shard_map/cond
Sparse Core Ops, SparseCore 0:
  9.6 45.7 all-gather.1
where the time goes:
time: 76.6 us; the launch traced here: 76.3 us
  waiting for transfers between devices  41.7 us (54%)
  between operations  14.1 us (18%)
  matrix products  10.6 us (14%)
  local copies, waits for them, and re-layouts  8.22 us (11%)
  other arithmetic  1.61 us (2%)
    all_gather x1, waiting for transfers between devices, body(): lax.all_gather(latents, 'ctx', axis=0, tiled=True)  41.7 us
    another operation x1, local copies, waits for them, and re-layouts  4.55 us
    dot_general x1, matrix products, body(): jnp.einsum('thl,hlc->thc', o_lat, w_uv, preferred_element_type=jnp.float32)  3.07 us
    dot_general x1, matrix products, body(): jnp.einsum('thi,hil->thl', shaped[:, :, :NOPE], w_uk, preferred_element_t...  2.86 us
    dot_general x1, matrix products, work(): jnp.einsum('thr,jr->thj', q_rope, block[:, RANK:], preferred_element_type...  1.96 us
    unnamed x1, local copies, waits for them, and re-layouts  1.7 us
  transfers between devices with their start and end apart: 1, of which 1 were waited for; matrix products, arithmetic and copies ran while one was open for 6% of the time, Pallas kernels for 0%

commit v1 on v0

--- a/solution.py
+++ b/solution.py
@@ -8,6 +8,12 @@
 ROPE = 64
 RANK = 512
 VDIM = 128
+
+
+def gather_from_all(x, axis, dim):
+    size = lax.axis_size(axis)
+    repeats = [size if d == dim else 1 for d in range(x.ndim)]
+    return lax.all_to_all(jnp.tile(x, repeats), axis, split_axis=dim, concat_axis=dim, tiled=True)
 
 
 def body(queries, latents, w_uk, w_uv):
@@ -73,9 +79,7 @@
         jnp.zeros((qrows, heads), jnp.float32),
         jnp.zeros((qrows, heads, RANK), jnp.float32),
     )
-    running, total, acc = accumulate(
-        init, lax.all_gather(latents, "ctx", axis=0, tiled=True), jnp.int32(0)
-    )
+    running, total, acc = accumulate(init, gather_from_all(latents, "ctx", 0), jnp.int32(0))
     o_lat = (acc / total[:, :, None]).astype(jnp.bfloat16)
     result = jnp.einsum("thl,hlc->thc", o_lat, w_uv, preferred_element_type=jnp.float32).astype(
         jnp.bfloat16

time: 76.6 us -> 75.7 us (0.988)
  the two profiles are of different devices: /device:TPU:0 before, /device:TPU:11 now
where the time goes in v1:
time: 75.7 us; the launch traced here: 75.4 us
  waiting for transfers between devices  48.5 us (64%)
  matrix products  9.64 us (13%)
  local copies, waits for them, and re-layouts  8.33 us (11%)
  starting transfers between devices  6.52 us (9%)
  other arithmetic  1.61 us (2%)
    all_to_all x1, waiting for transfers between devices, gather_from_all(): lax.all_to_all(jnp.tile(x, repeats), axis, split_axis=dim, concat_axis=di...  48.5 us
    all_to_all x1, starting transfers between devices, gather_from_all(): lax.all_to_all(jnp.tile(x, repeats), axis, split_axis=dim, concat_axis=di...  6.52 us
    another operation x1, local copies, waits for them, and re-layouts  3.09 us
    dot_general x1, matrix products, body(): jnp.einsum('thl,hlc->thc', o_lat, w_uv, preferred_element_type=jnp.float32)  3.07 us
    dot_general x1, matrix products, body(): jnp.einsum('thi,hil->thl', shaped[:, :, :NOPE], w_uk, preferred_element_t...  2.83 us
    another operation x1, local copies, waits for them, and re-layouts, gather_from_all(): jnp.tile(x, repeats)  2.82 us
  transfers between devices with their start and end apart: 1, of which 1 were waited for; matrix products, arithmetic and copies ran while one was open for 5% of the time, Pallas kernels for 0%

profile of v1, /device:TPU:11, one launch (start us, length us, event | category | flops | bytes accessed | tf_op | source)
XLA Modules:
  0.0 75.4 jit_solution(53422086097092464)
XLA Ops:
  0.0 0.0 copy-start.1
  0.0 2.8 %tile.2 = bf16[16,128,576]{1,2,0:T(8,128)(2,1)} broadcast(bf16[128,576]{0,1:T(8,128)(2,1)} %param.7), dimensions={1,2} | broadcast | bytes 2506752 | tf_op jit(solution)/shard_map/tile | solution.py:16
  2.8 6.5 %all-to-all-start = ((bf16[16,128,576]{1,2,0:T(8,128)(2,1)}), bf16[16,128,576]{1,2,0:T(8,128)(2,1)S(1)}, u32[]{:S(2)}, u32[]{:S(2)}) async-start(bf16[16,128,576]{1,2,0:T(8,128)(2,1)} %tile.2), calls=%async_computation | async-start | bytes 4718592 | tf_op jit(solution)/shard_map/all_to_all | solution.py:16
  9.3 0.6 fusion.16
  10.6 0.0 copy-done.1
  10.6 0.3 reshape.50
  11.0 2.8 %fusion.12 = bf16[16,32,512]{2,0,1:T(8,128)(2,1)S(1)} fusion(bf16[32,128,512]{2,1,0:T(8,128)(2,1)} %param.8, bf16[16,32,128]{2,1,0:T(8,128)(2,1)S(1)} %slice.17), kind=kOutput, calls=%fused_computation.17 | convolution fusion | flops 67371008 | bytes 4849664 | tf_op jit(solution)/shard_map/thi,hil->thl/dot_general | solution.py:27
  13.8 48.5 %all-to-all-done = bf16[16,128,576]{1,2,0:T(8,128)(2,1)S(1)} async-done(((bf16[16,128,576]{1,2,0:T(8,128)(2,1)}), bf16[16,128,576]{1,2,0:T(8,128)(2,1)S(1)}, u32[]{:S(2)}, u32[]{:S(2)}) %all-to-all-start) | async-done | bytes 2359328 | tf_op jit(solution)/shard_map/all_to_all | solution.py:16
  62.4 9.1 %conditional.1 = (f32[16,32]{1,0:T(8,128)S(1)}, f32[16,32,512]{2,1,0:T(8,128)S(1)}) conditional(s32[]{:T(128)} %convert_element_type.21, (s32[2048]{0:T(1024)S(1)}, s32[16]{0:T(128)S(1)}, bf16[16,128,576]{1,2,0:T(8,128)(2,1)S(1)}, bf16[16,32,512]{2,0,1:T(8,128)(2,1)S(1)}, bf16[16,32,192]{2,1,0:T(8,128)(2,1)S(1)}) %tuple.13, () %tuple.14), branch_computations={%region_1.4_spmd, %region_4.5_spmd} | conditional | flops 2290386432 | bytes 41658476 | solution.py:61
  62.4 0.0 copy-start
  62.4 1.4 %copy-done = bf16[16,128,576]{1,2,0:T(8,128)(2,1)} copy-done((bf16[16,128,576]{1,2,0:T(8,128)(2,1)}, bf16[16,128,576]{1,2,0:T(8,128)(2,1)S(1)}, u32[]{:S(2)}) %copy-start) | copy-done | bytes 2359320 | tf_op jit(solution)/shard_map/cond
  63.8 0.1 broadcast_compare_fusion
  63.9 3.1 %copy.18 = bf16[16,128,576]{2,1,0:T(8,128)(2,1)S(1)} copy(bf16[16,128,576]{1,2,0:T(8,128)(2,1)} %copy-done) | data formatting | bytes 4718592 | tf_op jit(solution)/shard_map
  67.0 1.4 %fusion.5 = f32[16,32,2048]{2,1,0:T(8,128)S(1)} fusion(bf16[2048,576]{1,0:T(8,128)(2,1)S(1)} %bitcast.22, bf16[16,32,512]{2,0,1:T(8,128)(2,1)S(1)} %get-tuple-element.39), kind=kOutput, calls=%fused_computation.7 | convolution fusion | flops 1073741824 | bytes 6815744 | tf_op jit(solution)/shard_map/cond/branch_0_fun/thl,jl->thj/dot_general | solution.py:40
  68.3 1.0 %fusion.17 = (f32[16,32]{1,0:T(8,128)S(1)}, f32[16,32,2048]{2,1,0:T(8,128)S(1)}) fusion(f32[16,32,2048]{2,1,0:T(8,128)S(1)} %fusion.5, bf16[2048,576]{1,0:T(8,128)(2,1)S(1)} %bitcast.23, bf16[16,32,192]{2,1,0:T(8,128)(2,1)S(1)} %get-tuple-element.21, pred[16,2048]{1,0:T(8,128)(4,1)S(1)} %broadcast_compare_fusion), kind=kOutput, calls=%fused_computation.26 | convolution fusion | flops 138411520 | bytes 9078784 | tf_op jit(solution)/shard_map/cond/branch_0_fun/thr,jr->thj/dot_general | solution.py:43
  69.4 0.7 fusion.1
  70.1 1.3 %fusion.6 = f32[16,32,512]{2,1,0:T(8,128)S(1)} fusion(bf16[2048,576]{1,0:T(8,128)(2,1)S(1)} %bitcast.24, f32[16,32,2048]{2,1,0:T(8,128)S(1)} %get-tuple-element.44, f32[16,32]{1,0:T(8,128)S(1)} %broadcast_maximum_fusion, f32[16,32]{1,0:T(8,128)S(1)} %get-tuple-element.41), kind=kOutput, calls=%fused_computation.8 | convolution fusion | flops 1076101120 | bytes 7356416 | tf_op jit(solution)/shard_map/cond/branch_0_fun/thj,jl->thl/dot_general | solution.py:53
  71.5 0.1 divide_convert_fusion
  71.6 3.1 %fusion.13 = bf16[32,2,8,128]{3,2,1,0:T(8,128)(2,1)S(1)} fusion(bf16[32,512,128]{2,1,0:T(8,128)(2,1)} %param.9, bf16[16,32,512]{2,1,0:T(8,128)(2,1)S(1)} %divide_convert_fusion), kind=kOutput, calls=%fused_computation.19 | convolution fusion | flops 67174400 | bytes 4849664 | tf_op jit(solution)/shard_map/thl,hlc->thc/dot_general | solution.py:84
  74.7 0.7 copy.33
  (5 shorter events, 0.0 us)
Async XLA Ops:
  0.0 10.6 %copy-start.1 = (bf16[16,6144]{1,0:T(8,128)(2,1)S(1)}, bf16[16,6144]{1,0:T(8,128)(2,1)}, u32[]{:S(2)}) copy-start(bf16[16,6144]{1,0:T(8,128)(2,1)} %param.6) | copy-start | bytes 589828
  2.8 59.6 %all-to-all-start = ((bf16[16,128,576]{1,2,0:T(8,128)(2,1)}), bf16[16,128,576]{1,2,0:T(8,128)(2,1)S(1)}, u32[]{:S(2)}, u32[]{:S(2)}) async-start(bf16[16,128,576]{1,2,0:T(8,128)(2,1)} %tile.2), calls=%async_computation | async-start | bytes 4718592 | tf_op jit(solution)/shard_map/all_to_all | solution.py:16
  62.4 1.4 %copy-start = (bf16[16,128,576]{1,2,0:T(8,128)(2,1)}, bf16[16,128,576]{1,2,0:T(8,128)(2,1)S(1)}, u32[]{:S(2)}) copy-start(bf16[16,128,576]{1,2,0:T(8,128)(2,1)S(1)} %get-tuple-element.38) | copy-start | bytes 7077892 | tf_op jit(solution)/shard_map/cond
